TPU v7x, 32 devices: a whole 2x2x4 slice. The times are simulated.
32 devices in a mesh: tp: 4 (over x, core), ep: 2 (over y), dp: 4 (over z).
Axes of the slice: x: 2, y: 2, z: 4, core: 2. Of those that a mesh axis runs over, the one named last changes fastest.
Arguments:
- tokens: bfloat16 [8, 512, 768], P(('ep', 'dp'), 'tp'), may hold values from -6 to 6
- segment: int32 [8, 512], P(('ep', 'dp')), may hold values from 0 to 7, never falling along the last dimension, each value on 1 to 256 neighbouring positions
- key_mask: int32 [8, 512], P(('ep', 'dp')), may hold values 0 or 1
- routes: int32 [8, 512, 2], P(('ep', 'dp'), 'tp'), may hold values from 0 to 3, all different within a row; in each aligned block of 128 rows (0 to 127, 128 to 255, ..., all dimensions but the last counted through in order) at most 128 rows name the same one
- gates: float32 [8, 512, 2], P(('ep', 'dp'), 'tp'), may hold values from 0.25 to 1
- ln1_gain: float32 [768], replicated, may hold values from 0.5 to 1.5
- ln1_bias: float32 [768], replicated, may hold values from -0.5 to 0.5
- query_weight: bfloat16 [768, 768], P(None, 'tp'), may hold values from -0.21875 to 0.21875
- key_weight: bfloat16 [768, 768], P(None, 'tp'), may hold values from -0.21875 to 0.21875
- value_weight: bfloat16 [768, 768], P(None, 'tp'), may hold values from -0.21875 to 0.21875
- out_weight: bfloat16 [768, 768], P('tp'), may hold values from -2.5 to 2.5
- ln2_gain: float32 [768], replicated, may hold values from 0.5 to 1.5
- ln2_bias: float32 [768], replicated, may hold values from -0.5 to 0.5
- frozen_in: bfloat16 [2, 768, 3072], P('ep'), may hold values from -0.21875 to 0.21875
- frozen_out: bfloat16 [2, 3072, 768], P('ep'), may hold values from -0.109375 to 0.109375
- train_in: bfloat16 [2, 768, 3072], P('ep'), may hold values from -0.21875 to 0.21875
- train_out: bfloat16 [2, 3072, 768], P('ep'), may hold values from -0.109375 to 0.109375
- cotangent: bfloat16 [8, 512, 768], P(('ep', 'dp'), 'tp'), may hold values from -6 to 6
Outputs:
- layer_out: bfloat16 [8, 512, 768], P(('ep', 'dp'), 'tp')
- tokens_grad: float32 [8, 512, 768], P(('ep', 'dp'), 'tp')
- ln1_gain_grad: float32 [768], replicated
- ln1_bias_grad: float32 [768], replicated
- query_grad: float32 [768, 768], P(None, 'tp')
- key_grad: float32 [768, 768], P(None, 'tp')
- value_grad: float32 [768, 768], P(None, 'tp')
- out_grad: float32 [768, 768], P('tp')
- ln2_gain_grad: float32 [768], replicated
- ln2_bias_grad: float32 [768], replicated
- train_in_grad: float32 [2, 768, 3072], P('ep')
- train_out_grad: float32 [2, 3072, 768], P('ep')
- expert_counts: int32 [4], replicated
Inputs may be any that keep to these rules, and one draw needn't show every extreme that they name: `segment`: segment numbers never fall along a group; each sequence holds 1 to 256 tokens, one exactly 256. `routes`: the two experts of a token differ. In the tokens of one device (aligned blocks of 128 tokens) no expert is named more than 128 times, a bound that some block reaches.
All inputs are finite; a program needn't handle non-finite values. No bound on the sum of `key_mask` on one device may be relied on, other than what follows from the above.
Results may differ from a plain program's by a relative error of at most 0.017.
Values may be sent and summed in bfloat16 or wider, within the bound.
A program may use at most 192 MiB of HBM per device.

v0:
```python
import jax
import jax.numpy as jnp
from jax import lax
from jax.sharding import PartitionSpec as P

HD = 64
EXP_DEV = 2
EPSILON = 1e-05
MASKED = -1e30


def layer_norm(values, gain, bias):
    center = jnp.mean(values, axis=-1, keepdims=True)
    shifted = values - center
    spread = jnp.mean(shifted * shifted, axis=-1, keepdims=True)
    return shifted * lax.rsqrt(spread + EPSILON) * gain + bias


def gelu_exact(values):
    return jax.nn.gelu(values, approximate=False)


def contract(left, right, left_dim, right_dim):
    return lax.dot_general(
        left, right, (((left_dim,), (right_dim,)), ((), ())), preferred_element_type=jnp.float32
    )


def masked_scores(queries, query_segment, keys, segment_row, keep_row):
    scale = queries.shape[-1] ** (-0.5)
    scores = jnp.einsum("hqd,hkd->hqk", queries, keys, preferred_element_type=jnp.float32) * scale
    allowed = (query_segment[:, None] == segment_row[None, :]) & keep_row[None, :]
    return jnp.where(allowed[None], scores, MASKED)


def to_owners(buffer):
    return lax.all_to_all(buffer, "ep", split_axis=0, concat_axis=0, tiled=True)


def to_sources(buffer):
    return lax.all_to_all(buffer, "ep", split_axis=0, concat_axis=0, tiled=True)


def expert_forward(inputs, inner, outer):
    hidden = contract(inputs, inner, 1, 0)
    active = gelu_exact(hidden).astype(jnp.bfloat16)
    return (hidden, active, contract(active, outer, 1, 0))


def expert_backward(inputs, hidden, active, upstream, inner, outer, trainable):
    through = contract(upstream, outer, 1, 1)
    slope = jax.vjp(gelu_exact, hidden)[1](through)[0].astype(jnp.bfloat16)
    back_in = contract(slope, inner, 1, 1)
    if trainable:
        return (back_in, contract(inputs, slope, 0, 0), contract(active, upstream, 0, 0))
    return (back_in, None, None)


def local(
    tokens,
    segment,
    key_mask,
    routes,
    gates,
    ln1_gain,
    ln1_bias,
    query_weight,
    key_weight,
    value_weight,
    out_weight,
    ln2_gain,
    ln2_bias,
    frozen_in,
    frozen_out,
    train_in,
    train_out,
    cotangent,
):
    tp_count = lax.axis_size("tp")
    ep_count = lax.axis_size("ep")
    local_rows = tokens.shape[1]
    width = tokens.shape[2]
    group_rows = local_rows * tp_count
    head_cols = query_weight.shape[1]
    local_heads = head_cols // HD
    residual = tokens[0].astype(jnp.float32)
    joined = jnp.concatenate([query_weight, key_weight, value_weight], axis=1)
    first_normed = layer_norm(residual, ln1_gain, ln1_bias).astype(jnp.bfloat16)
    piece = lax.all_gather(first_normed, "tp", axis=0, tiled=True)
    projected = contract(piece, joined, 1, 0)
    gathered = piece
    projected, normed_group = (projected, gathered)
    projected = projected.astype(jnp.bfloat16)
    block = min(512, group_rows)
    blocks = group_rows // block

    def split_heads(matrix):
        return matrix.reshape(group_rows, local_heads, HD).transpose(1, 0, 2)

    def merge_heads(tensor):
        return tensor.transpose(1, 0, 2).reshape(group_rows, head_cols)

    queries = split_heads(projected[:, :head_cols])
    keys = split_heads(projected[:, head_cols : 2 * head_cols])
    values = split_heads(projected[:, 2 * head_cols :])
    query_blocks = queries.reshape(local_heads, blocks, block, HD).transpose(1, 0, 2, 3)
    segment_row = segment[0]
    starts = jnp.concatenate(
        [segment_row[:1] == segment_row[:1], segment_row[1:] != segment_row[:-1]]
    )
    keep_row = (key_mask[0] == 1) | starts
    segment_blocks = segment_row.reshape(blocks, block)

    def forward_block(item):
        block_queries, block_segment = item
        scores = masked_scores(block_queries, block_segment, keys, segment_row, keep_row)
        highest = jnp.max(scores, axis=-1, keepdims=True)
        weights = jnp.exp(scores - highest)
        totals = jnp.sum(weights, axis=-1, keepdims=True)
        probs = (weights / totals).astype(jnp.bfloat16)
        outputs = jnp.einsum("hqk,hkd->hqd", probs, values, preferred_element_type=jnp.float32)
        return (outputs, (highest + jnp.log(totals))[..., 0])

    head_blocks, log_totals = lax.map(forward_block, (query_blocks, segment_blocks))
    attn_heads = (
        head_blocks.transpose(0, 2, 1, 3).reshape(group_rows, head_cols).astype(jnp.bfloat16)
    )
    middle = residual + lax.psum_scatter(
        contract(attn_heads, out_weight, 1, 0), "tp", scatter_dimension=0, tiled=True
    )
    second_normed = layer_norm(middle, ln2_gain, ln2_bias).astype(jnp.bfloat16)
    experts = EXP_DEV * ep_count
    capacity = 4 * local_rows // experts
    slots = experts * capacity
    route = routes[0]
    marks = (route.reshape(-1)[:, None] == jnp.arange(experts, dtype=jnp.int32)[None, :]).astype(
        jnp.int32
    )
    places = jnp.sum((jnp.cumsum(marks, axis=0) - 1) * marks, axis=1).reshape(local_rows, 2)
    slot_ids = route * capacity + places
    slot_range = jnp.arange(slots, dtype=jnp.int32)[None, :]
    pick_first = (slot_ids[:, 0:1] == slot_range).astype(jnp.bfloat16)
    pick_second = (slot_ids[:, 1:2] == slot_range).astype(jnp.bfloat16)
    local_counts = jnp.sum(marks, axis=0).astype(jnp.float32)
    send = contract(pick_first + pick_second, second_normed, 0, 0).astype(jnp.bfloat16)
    arrived = to_owners(send.reshape(ep_count, EXP_DEV, capacity, width))
    inner_list = (frozen_in[0], train_in[0])
    outer_list = (frozen_out[0], train_out[0])
    kept = []
    produced = []
    for index in range(EXP_DEV):
        inputs = arrived[:, index].reshape(-1, width)
        hidden, active, result = expert_forward(inputs, inner_list[index], outer_list[index])
        kept.append((inputs, hidden, active))
        produced.append(result.reshape(ep_count, -1, width))
    produced = jnp.stack(produced, axis=1)
    returned = to_sources(produced.astype(jnp.bfloat16)).reshape(slots, width)
    gate_rows = gates[0]
    mixture = gate_rows[:, 0:1] * contract(pick_first, returned, 1, 0) + gate_rows[
        :, 1:2
    ] * contract(pick_second, returned, 1, 0)
    layer_out = (middle + mixture).astype(jnp.bfloat16)
    upstream = cotangent[0].astype(jnp.float32)
    first_share = (gate_rows[:, 0:1] * upstream).astype(jnp.bfloat16)
    second_share = (gate_rows[:, 1:2] * upstream).astype(jnp.bfloat16)
    back_send = (
        contract(pick_first, first_share, 0, 0) + contract(pick_second, second_share, 0, 0)
    ).astype(jnp.bfloat16)
    back_arrived = to_owners(back_send.reshape(ep_count, EXP_DEV, capacity, width))
    input_terms = []
    grad_in = None
    grad_out = None
    for index in range(EXP_DEV):
        inputs, hidden, active = kept[index]
        back_in, maybe_in, maybe_out = expert_backward(
            inputs,
            hidden,
            active,
            back_arrived[:, index].reshape(-1, width),
            inner_list[index],
            outer_list[index],
            index == EXP_DEV - 1,
        )
        if index == EXP_DEV - 1:
            grad_in, grad_out = (maybe_in, maybe_out)
        input_terms.append(back_in.reshape(ep_count, -1, width))
    input_terms = jnp.stack(input_terms, axis=1)
    back_returned = to_sources(input_terms.astype(jnp.bfloat16)).reshape(slots, width)
    grad_in, grad_out = (
        lax.psum(grad_in.astype(jnp.bfloat16), ("tp", "dp")).astype(jnp.float32),
        lax.psum(grad_out.astype(jnp.bfloat16), ("tp", "dp")).astype(jnp.float32),
    )
    second_grad = contract(pick_first, back_returned, 1, 0) + contract(
        pick_second, back_returned, 1, 0
    )
    middle_part, ln2_gain_grad, ln2_bias_grad = jax.vjp(layer_norm, middle, ln2_gain, ln2_bias)[1](
        second_grad
    )
    middle_grad = upstream + middle_part
    attn_grad = middle_grad.astype(jnp.bfloat16)
    piece = lax.all_gather(attn_grad, "tp", axis=0, tiled=True)
    head_grad = contract(piece, out_weight, 1, 1)
    out_part = contract(attn_heads, piece, 0, 0)
    head_grad, out_part = (head_grad, out_part)
    upstream_blocks = (
        split_heads(head_grad.astype(jnp.bfloat16))
        .reshape(local_heads, blocks, block, HD)
        .transpose(1, 0, 2, 3)
    )

    def backward_block(carry, item):
        key_sum, value_sum = carry
        block_queries, block_segment, block_totals, block_upstream = item
        scores = masked_scores(block_queries, block_segment, keys, segment_row, keep_row)
        probs = jnp.exp(scores - block_totals[..., None])
        prob_grad = jnp.einsum(
            "hqd,hkd->hqk", block_upstream, values, preferred_element_type=jnp.float32
        )
        centered = jnp.sum(probs * prob_grad, axis=-1, keepdims=True)
        score_grad = (probs * (prob_grad - centered)).astype(jnp.bfloat16)
        scale = block_queries.shape[-1] ** (-0.5)
        query_part = (
            jnp.einsum("hqk,hkd->hqd", score_grad, keys, preferred_element_type=jnp.float32) * scale
        )
        key_sum = (
            key_sum
            + jnp.einsum(
                "hqk,hqd->hkd", score_grad, block_queries, preferred_element_type=jnp.float32
            )
            * scale
        )
        value_sum = value_sum + jnp.einsum(
            "hqk,hqd->hkd",
            probs.astype(jnp.bfloat16),
            block_upstream,
            preferred_element_type=jnp.float32,
        )
        return ((key_sum, value_sum), query_part)

    zero_heads = jnp.zeros((local_heads, group_rows, HD), jnp.float32)
    (key_sum, value_sum), query_parts = lax.scan(
        backward_block,
        (zero_heads, zero_heads),
        (query_blocks, segment_blocks, log_totals, upstream_blocks),
    )
    query_full = query_parts.transpose(0, 2, 1, 3).reshape(group_rows, head_cols)
    projected_grad = jnp.concatenate(
        [query_full, merge_heads(key_sum), merge_heads(value_sum)], axis=1
    ).astype(jnp.bfloat16)
    joined_grad = contract(normed_group, projected_grad, 0, 0)
    first_grad = lax.psum_scatter(
        contract(projected_grad, joined, 1, 1).astype(jnp.bfloat16),
        "tp",
        scatter_dimension=0,
        tiled=True,
    ).astype(jnp.float32)
    residual_part, ln1_gain_grad, ln1_bias_grad = jax.vjp(layer_norm, residual, ln1_gain, ln1_bias)[
        1
    ](first_grad)
    tokens_grad = middle_grad + residual_part
    summed = (
        lax.psum(joined_grad[:, :head_cols].astype(jnp.bfloat16), ("ep", "dp")).astype(jnp.float32),
        lax.psum(
            joined_grad[:, head_cols : 2 * head_cols].astype(jnp.bfloat16), ("ep", "dp")
        ).astype(jnp.float32),
        lax.psum(joined_grad[:, 2 * head_cols :].astype(jnp.bfloat16), ("ep", "dp")).astype(
            jnp.float32
        ),
        lax.psum(out_part.astype(jnp.bfloat16), ("ep", "dp")).astype(jnp.float32),
    )
    counts, gain_one, bias_one, gain_two, bias_two = lax.psum(
        (local_counts, ln1_gain_grad, ln1_bias_grad, ln2_gain_grad, ln2_bias_grad),
        ("tp", "ep", "dp"),
    )
    return (
        layer_out[None],
        tokens_grad[None],
        gain_one,
        bias_one,
        summed[0],
        summed[1],
        summed[2],
        summed[3],
        gain_two,
        bias_two,
        grad_in[None],
        grad_out[None],
        counts.astype(jnp.int32),
    )


def solution(mesh):
    in_specs = (
        P(("ep", "dp"), "tp", None),
        P(("ep", "dp"), None),
        P(("ep", "dp"), None),
        P(("ep", "dp"), "tp", None),
        P(("ep", "dp"), "tp", None),
        P(),
        P(),
        P(None, "tp"),
        P(None, "tp"),
        P(None, "tp"),
        P("tp", None),
        P(),
        P(),
        P("ep", None, None),
        P("ep", None, None),
        P("ep", None, None),
        P("ep", None, None),
        P(("ep", "dp"), "tp", None),
    )
    out_specs = (
        P(("ep", "dp"), "tp", None),
        P(("ep", "dp"), "tp", None),
        P(),
        P(),
        P(None, "tp"),
        P(None, "tp"),
        P(None, "tp"),
        P("tp", None),
        P(),
        P(),
        P("ep", None, None),
        P("ep", None, None),
        P(),
    )
    return jax.shard_map(local, mesh=mesh, in_specs=in_specs, out_specs=out_specs, check_vma=False)
```

profile of v0, /device:TPU:0, one launch (start us, length us, event | category | flops | bytes accessed | tf_op | source)
XLA Modules:
  0.0 457.1 jit_solution(4886164368282397368)
XLA Ops:
  9.9 1.1 fusion.84
  11.1 1.1 fusion.83
  12.2 10.1 %all_gather.6 = bf16[512,768]{1,0:T(8,128)(2,1)S(1)} all-gather(bf16[128,768]{1,0:T(8,128)(2,1)S(1)} %fusion.83), channel_id=1, replica_groups=mesh['tp'=4,'ep'=2,'dp'=4] {'tp'}, dimensions={0}, use_global_device_ids=true | all-gather | bytes 983040 | tf_op jit(solution)/shard_map/all_gather | solution.py:89
  22.3 1.2 constant_dynamic-update-slice_fusion.2
  29.4 1.6 fusion.132
  31.4 1.2 reduce-window.6
  34.9 1.4 fusion.91
  36.4 2.4 add_convert_fusion.2
  38.7 4.3 all-to-all-start.2
  43.0 16.9 %reduce-scatter.3.cloned.1.call-done = f32[128,768]{1,0:T(8,128)} async-done(((f32[512,768]{1,0:T(8,128)}), f32[128,768]{1,0:T(8,128)}) %reduce-scatter.3.cloned.1.call-update) | async-done | bytes 393232 | tf_op jit(solution)/shard_map/reduce_scatter | solution.py:128
  59.9 1.2 fusion.125
  61.8 1.4 convolution_convert_fusion.4
  63.2 4.5 all-to-all-start
  67.7 2.0 fusion.128
  69.8 8.8 %all-to-all-done = bf16[2,2,128,768]{3,2,1,0:T(8,128)(2,1)} async-done(((bf16[2,2,128,768]{3,2,1,0:T(8,128)(2,1)}), bf16[2,2,128,768]{3,2,1,0:T(8,128)(2,1)}, u32[]{:S(2)}, u32[]{:S(2)}) %all-to-all-start) | async-done | bytes 786464 | tf_op jit(solution)/shard_map/all_to_all | solution.py:37
  78.6 1.3 fusion.129
  80.0 11.0 %multiply_convert_fusion.2 = (bf16[256,3072]{1,0:T(8,128)(2,1)}, f32[256,3072]{1,0:T(8,128)S(1)}, f32[256,3072]{1,0:T(8,128)S(1)}) fusion(bf16[256,768]{1,0:T(8,128)(2,1)S(1)} %bitcast.231, bf16[1,768,3072]{2,1,0:T(8,128)(2,1)} %param.31), kind=kOutput, calls=%fused_computation.42 | convolution fusion | flops 1259077632 | bytes 12976128 | tf_op jit(solution)/shard_map/dot_general | solution.py:24
  91.0 2.0 add_convert_fusion.1
  93.1 1.4 fusion.55
  94.6 9.0 %multiply_convert_fusion.1 = (bf16[256,3072]{1,0:T(8,128)(2,1)}, f32[256,3072]{1,0:T(8,128)S(1)}, f32[256,3072]{1,0:T(8,128)S(1)}) fusion(bf16[256,768]{1,0:T(8,128)(2,1)S(1)} %bitcast.215, bf16[1,768,3072]{2,1,0:T(8,128)(2,1)S(1)} %bitcast.244), kind=kOutput, calls=%fused_computation.29 | convolution fusion | flops 1259077632 | bytes 12976128 | tf_op jit(solution)/shard_map/dot_general | solution.py:24
  103.6 2.0 add_convert_fusion
  105.6 1.4 fusion.52
  108.1 4.3 all-to-all-start.3
  112.5 10.1 %all-to-all-done.3 = bf16[2,2,128,768]{3,2,1,0:T(8,128)(2,1)} async-done(((bf16[2,2,128,768]{3,2,1,0:T(8,128)(2,1)}), bf16[2,2,128,768]{3,2,1,0:T(8,128)(2,1)}, u32[]{:S(2)}, u32[]{:S(2)}) %all-to-all-start.3) | async-done | bytes 786464 | tf_op jit(solution)/shard_map/all_to_all | solution.py:41
  122.6 1.5 fusion.90
  124.1 1.7 multiply_reduce_fusion.1
  126.9 7.8 %all_gather.7 = bf16[512,768]{1,0:T(8,128)(2,1)S(1)} all-gather(bf16[128,768]{1,0:T(8,128)(2,1)S(1)} %fusion.94), channel_id=1, replica_groups=mesh['tp'=4,'ep'=2,'dp'=4] {'tp'}, dimensions={0}, use_global_device_ids=true | all-gather | bytes 983040 | tf_op jit(solution)/shard_map/all_gather | solution.py:201
  141.2 2.7 convolution_convert_fusion.3
  144.2 5.2 %fusion.16 = bf16[1,768,3072]{2,1,0:T(8,128)(2,1)} fusion(bf16[256,768]{1,0:T(8,128)(2,1)S(1)} %bitcast.216, bf16[256,3072]{1,0:T(8,128)(2,1)} %copy-done.19), kind=kOutput, calls=%fused_computation.20 | convolution fusion | flops 1210318848 | bytes 6684672 | tf_op jit(solution)/shard_map/dot_general | solution.py:24
  149.4 3.6 fusion.17
  153.1 1.4 copy-done.37
  154.5 3.7 fusion.61
  158.2 3.8 fusion.58
  163.0 3.5 all-to-all-start.1
  166.6 13.7 %all-to-all-done.1 = bf16[2,2,128,768]{3,2,1,0:T(8,128)(2,1)S(1)} async-done(((bf16[2,2,128,768]{3,2,1,0:T(8,128)(2,1)}), bf16[2,2,128,768]{3,2,1,0:T(8,128)(2,1)S(1)}, u32[]{:S(2)}, u32[]{:S(2)}) %all-to-all-start.1) | async-done | bytes 786464 | tf_op jit(solution)/shard_map/all_to_all | solution.py:41
  181.6 42.1 %all-reduce.9.cloned.1.call-done = (bf16[768,192]{0,1:T(8,128)(2,1)}, bf16[768,192]{0,1:T(8,128)(2,1)}, bf16[768,192]{0,1:T(8,128)(2,1)}, bf16[192,768]{1,0:T(8,128)(2,1)}) async-done(((bf16[768,192]{0,1:T(8,128)(2,1)}, bf16[768,192]{0,1:T(8,128)(2,1)}, bf16[768,192]{0,1:T(8,128)(2,1)}, bf16[192,768]{1,0:T(8,128)(2,1)}), (bf16[768,192]{0,1:T(8,128)(2,1)}, bf16[768,192]{0,1:T(8,128)(2,1)}, ...) | async-done | bytes 1179664 | tf_op jit(solution)/shard_map/psum | solution.py:262
  223.7 1.8 convert_element_type.162
  225.5 1.8 convert_element_type.163
  227.3 1.8 convert_element_type.164
  229.1 1.8 convert_element_type.166
  230.9 17.7 %reduce-scatter.5.cloned.1.call-done = bf16[128,768]{1,0:T(8,128)(2,1)} async-done(((bf16[512,768]{1,0:T(8,128)(2,1)}), bf16[128,768]{1,0:T(8,128)(2,1)}) %reduce-scatter.5.cloned.1.call-update) | async-done | bytes 196624 | tf_op jit(solution)/shard_map/reduce_scatter | solution.py:251
  248.6 1.1 convert_reduce_fusion
  249.8 1.2 fusion.86
  251.0 41.6 %all-reduce.1 = (f32[768]{0:T(1024)}, f32[768]{0:T(1024)}, f32[768]{0:T(1024)}, f32[768]{0:T(1024)}, f32[4]{0:T(128)S(1)}) all-reduce(f32[768]{0:T(1024)S(1)} %get-tuple-element.61, f32[768]{0:T(1024)S(1)} %get-tuple-element.64, f32[768]{0:T(1024)S(1)} %get-tuple-element.59, ...), channel_id=1, replica_groups=mesh['tp'=4,'ep'=2,'dp'=4] {'tp','ep','dp'}, use_global_device_ids=true, to_apply=%region_17.18 | all-reduce | flops 3076 | bytes 24608 | tf_op jit(solution)/shard_map/psum | solution.py:271
  293.2 1.9 add_bitcast_fusion
  295.1 143.5 %all-reduce.7.cloned.1.call-done = (bf16[1,768,3072]{2,1,0:T(8,128)(2,1)}, bf16[1,3072,768]{2,1,0:T(8,128)(2,1)}) async-done(((bf16[1,768,3072]{2,1,0:T(8,128)(2,1)}, bf16[1,3072,768]{2,1,0:T(8,128)(2,1)}), (bf16[1,768,3072]{2,1,0:T(8,128)(2,1)}, bf16[1,3072,768]{2,1,0:T(8,128)(2,1)})) %all-reduce.7.cloned.1.call-update) | async-done | bytes 9437200 | tf_op jit(solution)/shard_map/psum | solution.py:190
  438.5 7.5 %broadcast_in_dim.113 = f32[1,768,3072]{2,1,0:T(8,128)} convert(bf16[1,768,3072]{2,1,0:T(8,128)(2,1)} %get-tuple-element.86) | non-fusion elementwise | flops 2359296 | bytes 14155776 | tf_op jit(solution)/shard_map/broadcast_in_dim | solution.py:286
  446.1 4.5 broadcast_in_dim.115
  (160 shorter events, 23.9 us)
Async XLA Ops:
  7.2 22.2 %copy-start = (bf16[192,768]{1,0:T(8,128)(2,1)S(1)}, bf16[192,768]{1,0:T(8,128)(2,1)}, u32[]{:S(2)}) copy-start(bf16[192,768]{1,0:T(8,128)(2,1)} %param.28) | copy-start | bytes 884740
  7.2 17.2 %copy-start.27 = (bf16[768,192]{0,1:T(8,128)(2,1)S(1)}, bf16[768,192]{0,1:T(8,128)(2,1)}, u32[]{:S(2)}) copy-start(bf16[768,192]{0,1:T(8,128)(2,1)} %param.27) | copy-start | bytes 884740
  7.2 52.7 %reduce-scatter.3.cloned.1.call-start = ((), (), s32[]{:S(2)}) async-start(), calls=%async_computation.6 | async-start | bytes 1966080 | tf_op jit(solution)/shard_map/reduce_scatter | solution.py:128
  12.2 14.0 %copy-start.33 = (s32[1,512]{1,0:T(1,128)S(1)}, s32[1,512]{1,0:T(1,128)}, u32[]{:S(2)}) copy-start(s32[1,512]{1,0:T(1,128)} %param.19) | copy-start | bytes 6148
  22.3 4.2 copy-start.22
  26.1 1.4 copy-start.15
  26.1 1.9 copy-start.20
  28.7 2.3 copy-start.35
  28.7 6.2 %copy-start.36 = (f32[1,128,2]{1,2,0:T(2,128)S(1)}, f32[1,128,2]{1,2,0:T(2,128)}, u32[]{:S(2)}) copy-start(f32[1,128,2]{1,2,0:T(2,128)} %param.22) | copy-start | bytes 3076
  36.3 25.5 %copy-start.32 = (f32[768]{0:T(1024)S(1)}, f32[768]{0:T(1024)}, u32[]{:S(2)}) copy-start(f32[768]{0:T(1024)} %param.29) | copy-start | bytes 9220
  36.3 25.5 %copy-start.34 = (f32[768]{0:T(1024)S(1)}, f32[768]{0:T(1024)}, u32[]{:S(2)}) copy-start(f32[768]{0:T(1024)} %param.30) | copy-start | bytes 9220
  38.7 24.5 %all-to-all-start.2 = ((bf16[2,2,128,768]{3,2,1,0:T(8,128)(2,1)}), bf16[2,2,128,768]{3,2,1,0:T(8,128)(2,1)}, u32[]{:S(2)}, u32[]{:S(2)}) async-start(bf16[2,2,128,768]{3,2,1,0:T(8,128)(2,1)} %bitcast.214), calls=%async_computation.3 | async-start | bytes 1572864 | tf_op jit(solution)/shard_map/all_to_all | solution.py:37
  63.2 15.3 %all-to-all-start = ((bf16[2,2,128,768]{3,2,1,0:T(8,128)(2,1)}), bf16[2,2,128,768]{3,2,1,0:T(8,128)(2,1)}, u32[]{:S(2)}, u32[]{:S(2)}) async-start(bf16[2,2,128,768]{3,2,1,0:T(8,128)(2,1)} %bitcast.213), calls=%async_computation.1 | async-start | bytes 1572864 | tf_op jit(solution)/shard_map/all_to_all | solution.py:37
  78.6 12.4 %slice-start.4 = ((s8[4718592]{0:T(1024)(128)(4,1)}), s8[4194304]{0:T(1024)(128)(4,1)S(1)}, s32[]{:S(2)}) async-start(s8[4718592]{0:T(1024)(128)(4,1)} %bitcast.245), calls=%async_computation.14 | async-start | bytes 8388608
  78.6 14.5 %slice-start = ((s8[4718592]{0:T(1024)(128)(4,1)}), s8[4194304]{0:T(1024)(128)(4,1)S(1)}, s32[]{:S(2)}) async-start(s8[4718592]{0:T(1024)(128)(4,1)} %bitcast.241), calls=%async_computation.10 | async-start | bytes 8388608
  78.6 15.9 %slice-start.2 = ((s8[4718592]{0:T(1024)(128)(4,1)}), s8[4194304]{0:T(1024)(128)(4,1)S(1)}, s32[]{:S(2)}) async-start(s8[4718592]{0:T(1024)(128)(4,1)} %bitcast.243), calls=%async_computation.12 | async-start | bytes 8388608
  79.9 14.6 %copy-start.11 = (bf16[2,1,128,768]{3,2,1,0:T(8,128)(2,1)}, bf16[2,1,128,768]{3,2,1,0:T(8,128)(2,1)S(1)}, u32[]{:S(2)}) copy-start(bf16[2,1,128,768]{3,2,1,0:T(8,128)(2,1)S(1)} %get-tuple-element.106) | copy-start | bytes 1179652
  79.9 11.1 %copy-start.26 = (bf16[2,1,128,768]{3,2,1,0:T(8,128)(2,1)S(1)}, bf16[2,1,128,768]{3,2,1,0:T(8,128)(2,1)}, u32[]{:S(2)}) copy-start(bf16[2,1,128,768]{3,2,1,0:T(8,128)(2,1)} %get-tuple-element.103) | copy-start | bytes 1179652
  79.9 11.1 %slice-start.5 = ((s8[4718592]{0:T(1024)(128)(4,1)}), s8[524288]{0:T(1024)(128)(4,1)S(1)}, s32[]{:S(2)}) async-start(s8[4718592]{0:T(1024)(128)(4,1)} %bitcast.245), calls=%async_computation.15 | async-start | bytes 1048576
  79.9 13.1 %slice-start.1 = ((s8[4718592]{0:T(1024)(128)(4,1)}), s8[524288]{0:T(1024)(128)(4,1)S(1)}, s32[]{:S(2)}) async-start(s8[4718592]{0:T(1024)(128)(4,1)} %bitcast.241), calls=%async_computation.11 | async-start | bytes 1048576
  79.9 14.6 %slice-start.3 = ((s8[4718592]{0:T(1024)(128)(4,1)}), s8[524288]{0:T(1024)(128)(4,1)S(1)}, s32[]{:S(2)}) async-start(s8[4718592]{0:T(1024)(128)(4,1)} %bitcast.243), calls=%async_computation.13 | async-start | bytes 1048576
  93.0 10.5 %slice-start.6 = ((s8[4718592]{0:T(1024)(128)(4,1)}), s8[4194304]{0:T(1024)(128)(4,1)S(1)}, s32[]{:S(2)}) async-start(s8[4718592]{0:T(1024)(128)(4,1)} %bitcast.247), calls=%async_computation.16 | async-start | bytes 8388608
  94.5 9.0 %copy-start.17 = (bf16[2,1,128,768]{3,2,1,0:T(8,128)(2,1)S(1)}, bf16[2,1,128,768]{3,2,1,0:T(8,128)(2,1)}, u32[]{:S(2)}) copy-start(bf16[2,1,128,768]{3,2,1,0:T(8,128)(2,1)} %get-tuple-element.104) | copy-start | bytes 1179652
  94.5 9.0 %slice-start.7 = ((s8[4718592]{0:T(1024)(128)(4,1)}), s8[524288]{0:T(1024)(128)(4,1)S(1)}, s32[]{:S(2)}) async-start(s8[4718592]{0:T(1024)(128)(4,1)} %bitcast.247), calls=%async_computation.17 | async-start | bytes 1048576
  105.6 1.5 copy-start.19
  108.1 14.5 %all-to-all-start.3 = ((bf16[2,2,128,768]{3,2,1,0:T(8,128)(2,1)}), bf16[2,2,128,768]{3,2,1,0:T(8,128)(2,1)}, u32[]{:S(2)}, u32[]{:S(2)}) async-start(bf16[2,2,128,768]{3,2,1,0:T(8,128)(2,1)} %copy.66), calls=%async_computation.4 | async-start | bytes 1572864 | tf_op jit(solution)/shard_map/all_to_all | solution.py:41
  112.4 111.2 %all-reduce.9.cloned.1.call-start = ((), (), s32[]{:S(2)}) async-start(), calls=%async_computation.9 | async-start | bytes 2359296 | tf_op jit(solution)/shard_map/psum | solution.py:262
  122.6 3.2 copy-start.2
  122.6 4.2 copy-start.9
  122.6 12.1 %copy-start.25 = (bf16[3,512,64]{1,2,0:T(8,128)(2,1)S(1)}, bf16[3,512,64]{1,2,0:T(8,128)(2,1)}, u32[]{:S(2)}) copy-start(bf16[3,512,64]{1,2,0:T(8,128)(2,1)} %copy-done.24) | copy-start | bytes 589828
  134.7 2.1 copy-start.21
  136.8 2.7 copy-start.28
  137.5 1.5 copy-start.14
  138.4 1.2 copy-start.23
  139.6 1.6 copy-start.30
  141.1 3.1 copy-start.12
  141.2 107.5 %reduce-scatter.5.cloned.1.call-start = ((), (), s32[]{:S(2)}) async-start(), calls=%async_computation.7 | async-start | bytes 983040 | tf_op jit(solution)/shard_map/reduce_scatter | solution.py:251
  143.9 5.5 %copy-start.6 = (bf16[256,3072]{1,0:T(8,128)(2,1)S(1)}, bf16[256,3072]{1,0:T(8,128)(2,1)}, u32[]{:S(2)}) copy-start(bf16[256,3072]{1,0:T(8,128)(2,1)} %get-tuple-element.96) | copy-start | bytes 4718596
  143.9 5.5 %copy-start.18 = (bf16[2,1,128,768]{3,2,1,0:T(8,128)(2,1)S(1)}, bf16[2,1,128,768]{3,2,1,0:T(8,128)(2,1)}, u32[]{:S(2)}) copy-start(bf16[2,1,128,768]{3,2,1,0:T(8,128)(2,1)} %get-tuple-element.104) | copy-start | bytes 1179652
  143.9 294.6 %all-reduce.7.cloned.1.call-start = ((), (), s32[]{:S(2)}) async-start(), calls=%async_computation.8 | async-start | bytes 18874368 | tf_op jit(solution)/shard_map/psum | solution.py:190
  153.1 1.4 copy-start.37
  162.0 18.6 %copy-start.3 = (f32[128,768]{1,0:T(8,128)S(1)}, f32[128,768]{1,0:T(8,128)}, u32[]{:S(2)}) copy-start(f32[128,768]{1,0:T(8,128)} %copy-done.1) | copy-start | bytes 1179652
  163.0 17.2 %all-to-all-start.1 = ((bf16[2,2,128,768]{3,2,1,0:T(8,128)(2,1)}), bf16[2,2,128,768]{3,2,1,0:T(8,128)(2,1)S(1)}, u32[]{:S(2)}, u32[]{:S(2)}) async-start(bf16[2,2,128,768]{3,2,1,0:T(8,128)(2,1)} %copy.65), calls=%async_computation.2 | async-start | bytes 1572864 | tf_op jit(solution)/shard_map/all_to_all | solution.py:41
  180.2 68.4 %copy-start.4 = (bf16[1,128,768]{2,1,0:T(8,128)(2,1)S(1)}, bf16[1,128,768]{2,1,0:T(8,128)(2,1)}, u32[]{:S(2)}) copy-start(bf16[1,128,768]{2,1,0:T(8,128)(2,1)} %param.18) | copy-start | bytes 589828
  180.2 68.4 %copy-start.31 = (f32[768]{0:T(1024)S(1)}, f32[768]{0:T(1024)}, u32[]{:S(2)}) copy-start(f32[768]{0:T(1024)} %param.23) | copy-start | bytes 9220
  180.6 112.6 %copy-start.8 = (f32[128,768]{1,0:T(8,128)S(1)}, f32[128,768]{1,0:T(8,128)}, u32[]{:S(2)}) copy-start(f32[128,768]{1,0:T(8,128)} %copy-done.7) | copy-start | bytes 1179652
  180.6 112.6 %copy-start.10 = (bf16[1,128,768]{2,1,0:T(8,128)(2,1)S(1)}, bf16[1,128,768]{2,1,0:T(8,128)(2,1)}, u32[]{:S(2)}) copy-start(bf16[1,128,768]{2,1,0:T(8,128)(2,1)} %param.35) | copy-start | bytes 589828
  438.5 7.5 %copy-start.5 = (bf16[1,3072,768]{2,1,0:T(8,128)(2,1)S(1)}, bf16[1,3072,768]{2,1,0:T(8,128)(2,1)}, u32[]{:S(2)}) copy-start(bf16[1,3072,768]{2,1,0:T(8,128)(2,1)} %get-tuple-element.87) | copy-start | bytes 14155780
  (6 other events, 4.7 us)
Sparse Core Ops, SparseCore 0:
  31.1 28.8 reduce-scatter.2
  141.3 82.3 all-reduce.8
  226.2 22.3 reduce-scatter.4
  252.8 185.7 all-reduce.6
where the time goes:
time: 458 us; the launch traced here: 457 us
  waiting for transfers between devices  253 us (55%)
  matrix products  63.5 us (14%)
  blocking collectives  59.5 us (13%)
  other arithmetic  34.8 us (8%)
  starting transfers between devices  17.1 us (4%)
  local copies, waits for them, and re-layouts  14.9 us (3%)
  between operations  14.5 us (3%)
    psum x1, waiting for transfers between devices, local(): lax.psum(grad_in.astype(jnp.bfloat16), ('tp', 'dp')).astype(jnp.float32)  143 us
    dot_general x23, matrix products, contract(): lax.dot_general(left, right, (((left_dim,), (right_dim,)), ((), ())), pre...  59.8 us
    psum x1, waiting for transfers between devices, local(): lax.psum(joined_grad[:, :head_cols].astype(jnp.bfloat16), ('ep', 'dp'))  42.1 us
    psum x1, blocking collectives, local(): lax.psum((local_counts, ln1_gain_grad, ln1_bias_grad, ln2_gain_grad, ln2_...  41.6 us
    all_to_all x2, waiting for transfers between devices, to_sources(): return lax.all_to_all(buffer, 'ep', split_axis=0, concat_axis=0, tiled=True)  23.7 us
    reduce_scatter x1, waiting for transfers between devices, local(): lax.psum_scatter(contract(projected_grad, joined, 1, 1).astype(jnp.bfloat...  17.7 us
    reduce_scatter x1, waiting for transfers between devices, local(): lax.psum_scatter(contract(attn_heads, out_weight, 1, 0), 'tp', scatter_di...  16.9 us
    all_gather x1, blocking collectives, local(): piece = lax.all_gather(first_normed, 'tp', axis=0, tiled=True)  10.1 us
  transfers between devices with their start and end apart: 8, of which 7 were waited for; matrix products, arithmetic and copies ran while one was open for 10% of the time, Pallas kernels for 0%

commit v1 on v0

--- a/solution.py
+++ b/solution.py
@@ -1,3 +1,4 @@
+import functools
 import jax
 import jax.numpy as jnp
 from jax import lax
@@ -7,6 +8,13 @@
 EXP_DEV = 2
 EPSILON = 1e-05
 MASKED = -1e30
+
+
+def point_works_now(in_array, ax_name):
+    return jnp.sum(lax.all_gather(in_array, ax_name), 0)
+
+
+supply_all_the_halves = functools.partial(point_works_now, ax_name=("ep", "dp"))
 
 
 def layer_norm(values, gain, bias):
@@ -259,7 +267,7 @@
     ](first_grad)
     tokens_grad = middle_grad + residual_part
     summed = (
-        lax.psum(joined_grad[:, :head_cols].astype(jnp.bfloat16), ("ep", "dp")).astype(jnp.float32),
+        supply_all_the_halves(joined_grad[:, :head_cols].astype(jnp.bfloat16)).astype(jnp.float32),
         lax.psum(
             joined_grad[:, head_cols : 2 * head_cols].astype(jnp.bfloat16), ("ep", "dp")
         ).astype(jnp.float32),

time: 458 us -> 505 us (1.10)
  waiting for transfers between devices: 253 us -> 296 us
    psum x1, waiting for transfers between devices: 143 us -> 182 us  [local(): lax.psum(grad_in.astype(jnp.bfloat16), ('tp', 'dp')).astype(jnp.float32)]
    all_gather x0 -> x1, waiting for transfers between devices: none -> 8.33 us  [point_works_now(): return jnp.sum(lax.all_gather(in_array, ax_name), 0)]
  transfers between devices with their start and end apart: 8 -> 9, of which waited for: 7 -> 8; matrix products, arithmetic and copies ran while one was open for 10% -> 10% of each run, Pallas kernels for 0% -> 0%
where the time goes in v1:
time: 505 us; the launch traced here: 504 us
  waiting for transfers between devices  296 us (59%)
  matrix products  63.6 us (13%)
  blocking collectives  59.8 us (12%)
  other arithmetic  35.5 us (7%)
  local copies, waits for them, and re-layouts  17.2 us (3%)
  starting transfers between devices  17.1 us (3%)
  between operations  14.6 us (3%)
    psum x1, waiting for transfers between devices, local(): lax.psum(grad_in.astype(jnp.bfloat16), ('tp', 'dp')).astype(jnp.float32)  182 us
    dot_general x23, matrix products, contract(): lax.dot_general(left, right, (((left_dim,), (right_dim,)), ((), ())), pre...  59.9 us
    psum x1, blocking collectives, local(): lax.psum((local_counts, ln1_gain_grad, ln1_bias_grad, ln2_gain_grad, ln2_...  41.9 us
    psum x1, waiting for transfers between devices, local(): lax.psum(joined_grad[:, head_cols:2 * head_cols].astype(jnp.bfloat16), ('...  37.9 us
    all_to_all x2, waiting for transfers between devices, to_sources(): return lax.all_to_all(buffer, 'ep', split_axis=0, concat_axis=0, tiled=True)  21.6 us
    reduce_scatter x1, waiting for transfers between devices, local(): lax.psum_scatter(contract(projected_grad, joined, 1, 1).astype(jnp.bfloat...  19.2 us
    reduce_scatter x1, waiting for transfers between devices, local(): lax.psum_scatter(contract(attn_heads, out_weight, 1, 0), 'tp', scatter_di...  16.9 us
  transfers between devices with their start and end apart: 9, of which 8 were waited for; matrix products, arithmetic and copies ran while one was open for 10% of the time, Pallas kernels for 0%

profile of v1, /device:TPU:0, one launch (start us, length us, event | category | flops | bytes accessed | tf_op | source)
XLA Modules:
  0.0 503.5 jit_solution(13059932257525367750)
XLA Ops:
  12.2 10.1 %all_gather.12 = bf16[512,768]{1,0:T(8,128)(2,1)S(1)} all-gather(bf16[128,768]{1,0:T(8,128)(2,1)S(1)} %fusion.83), channel_id=1, replica_groups=mesh['tp'=4,'ep'=2,'dp'=4] {'tp'}, dimensions={0}, use_global_device_ids=true | all-gather | bytes 983040 | tf_op jit(solution)/shard_map/all_gather | solution.py:97
  22.3 1.2 constant_dynamic-update-slice_fusion.2
  29.4 1.6 fusion.132
  31.3 1.2 reduce-window.6
  34.9 1.4 fusion.91
  36.4 2.4 add_convert_fusion.2
  38.7 4.3 all-to-all-start.2
  43.0 16.9 %reduce-scatter.3.cloned.1.call-done = f32[128,768]{1,0:T(8,128)} async-done(((f32[512,768]{1,0:T(8,128)}), f32[128,768]{1,0:T(8,128)}) %reduce-scatter.3.cloned.1.call-update) | async-done | bytes 393232 | tf_op jit(solution)/shard_map/reduce_scatter | solution.py:136
  59.9 1.2 fusion.125
  61.8 1.4 convolution_convert_fusion.4
  63.2 4.5 all-to-all-start
  67.7 2.0 fusion.128
  69.8 8.8 %all-to-all-done = bf16[2,2,128,768]{3,2,1,0:T(8,128)(2,1)} async-done(((bf16[2,2,128,768]{3,2,1,0:T(8,128)(2,1)}), bf16[2,2,128,768]{3,2,1,0:T(8,128)(2,1)}, u32[]{:S(2)}, u32[]{:S(2)}) %all-to-all-start) | async-done | bytes 786464 | tf_op jit(solution)/shard_map/all_to_all | solution.py:45
  78.6 1.3 fusion.129
  79.9 11.0 %multiply_convert_fusion.2 = (bf16[256,3072]{1,0:T(8,128)(2,1)}, f32[256,3072]{1,0:T(8,128)S(1)}, f32[256,3072]{1,0:T(8,128)S(1)}) fusion(bf16[256,768]{1,0:T(8,128)(2,1)S(1)} %bitcast.237, bf16[1,768,3072]{2,1,0:T(8,128)(2,1)} %param.31), kind=kOutput, calls=%fused_computation.42 | convolution fusion | flops 1259077632 | bytes 12976128 | tf_op jit(solution)/shard_map/dot_general | solution.py:32
  91.0 2.1 add_convert_fusion.1
  93.1 1.4 fusion.55
  94.6 9.0 %multiply_convert_fusion.1 = (bf16[256,3072]{1,0:T(8,128)(2,1)}, f32[256,3072]{1,0:T(8,128)S(1)}, f32[256,3072]{1,0:T(8,128)S(1)}) fusion(bf16[256,768]{1,0:T(8,128)(2,1)S(1)} %bitcast.221, bf16[1,768,3072]{2,1,0:T(8,128)(2,1)S(1)} %bitcast.250), kind=kOutput, calls=%fused_computation.29 | convolution fusion | flops 1259077632 | bytes 12976128 | tf_op jit(solution)/shard_map/dot_general | solution.py:32
  103.6 2.0 add_convert_fusion
  105.6 1.4 fusion.52
  108.1 4.3 all-to-all-start.3
  112.5 10.0 %all-to-all-done.3 = bf16[2,2,128,768]{3,2,1,0:T(8,128)(2,1)} async-done(((bf16[2,2,128,768]{3,2,1,0:T(8,128)(2,1)}), bf16[2,2,128,768]{3,2,1,0:T(8,128)(2,1)}, u32[]{:S(2)}, u32[]{:S(2)}) %all-to-all-start.3) | async-done | bytes 786464 | tf_op jit(solution)/shard_map/all_to_all | solution.py:49
  122.6 1.5 fusion.90
  124.1 1.7 multiply_reduce_fusion.1
  126.9 7.8 %all_gather.13 = bf16[512,768]{1,0:T(8,128)(2,1)S(1)} all-gather(bf16[128,768]{1,0:T(8,128)(2,1)S(1)} %fusion.94), channel_id=1, replica_groups=mesh['tp'=4,'ep'=2,'dp'=4] {'tp'}, dimensions={0}, use_global_device_ids=true | all-gather | bytes 983040 | tf_op jit(solution)/shard_map/all_gather | solution.py:209
  141.2 2.7 convolution_convert_fusion.3
  144.8 5.2 %fusion.16 = bf16[1,768,3072]{2,1,0:T(8,128)(2,1)} fusion(bf16[256,768]{1,0:T(8,128)(2,1)S(1)} %bitcast.222, bf16[256,3072]{1,0:T(8,128)(2,1)} %copy-done.19), kind=kOutput, calls=%fused_computation.20 | convolution fusion | flops 1210318848 | bytes 6684672 | tf_op jit(solution)/shard_map/dot_general | solution.py:32
  150.0 3.6 fusion.17
  153.7 1.4 copy-done.37
  155.1 3.8 fusion.61
  158.8 3.8 fusion.58
  163.6 3.6 all-to-all-start.1
  167.2 11.5 %all-to-all-done.1 = bf16[2,2,128,768]{3,2,1,0:T(8,128)(2,1)S(1)} async-done(((bf16[2,2,128,768]{3,2,1,0:T(8,128)(2,1)}), bf16[2,2,128,768]{3,2,1,0:T(8,128)(2,1)S(1)}, u32[]{:S(2)}, u32[]{:S(2)}) %all-to-all-start.1) | async-done | bytes 786464 | tf_op jit(solution)/shard_map/all_to_all | solution.py:49
  180.1 37.9 %all-reduce.9.cloned.1.call-done = (bf16[768,192]{0,1:T(8,128)(2,1)}, bf16[768,192]{0,1:T(8,128)(2,1)}, bf16[192,768]{1,0:T(8,128)(2,1)}) async-done(((bf16[768,192]{0,1:T(8,128)(2,1)}, bf16[768,192]{0,1:T(8,128)(2,1)}, bf16[192,768]{1,0:T(8,128)(2,1)}), (bf16[768,192]{0,1:T(8,128)(2,1)}, bf16[768,192]{0,1:T(8,128)(2,1)}, bf16[192,768]{1,0:T(8,128)(2,1)})) %all-reduce.9.cloned.1.call-update) | async-done | bytes 884752 | tf_op jit(solution)/shard_map/psum | solution.py:271
  218.0 1.8 convert_element_type.165
  219.8 1.8 convert_element_type.166
  221.6 1.8 convert_element_type.168
  223.5 19.2 %reduce-scatter.5.cloned.1.call-done = bf16[128,768]{1,0:T(8,128)(2,1)} async-done(((bf16[512,768]{1,0:T(8,128)(2,1)}), bf16[128,768]{1,0:T(8,128)(2,1)}) %reduce-scatter.5.cloned.1.call-update) | async-done | bytes 196624 | tf_op jit(solution)/shard_map/reduce_scatter | solution.py:259
  242.7 1.1 convert_reduce_fusion
  243.9 1.2 fusion.86
  245.1 41.9 %all-reduce.1 = (f32[768]{0:T(1024)}, f32[768]{0:T(1024)}, f32[768]{0:T(1024)}, f32[768]{0:T(1024)}, f32[4]{0:T(128)S(1)}) all-reduce(f32[768]{0:T(1024)S(1)} %get-tuple-element.61, f32[768]{0:T(1024)S(1)} %get-tuple-element.64, f32[768]{0:T(1024)S(1)} %get-tuple-element.59, ...), channel_id=1, replica_groups=mesh['tp'=4,'ep'=2,'dp'=4] {'tp','ep','dp'}, use_global_device_ids=true, to_apply=%region_17.18 | all-reduce | flops 3076 | bytes 24608 | tf_op jit(solution)/shard_map/psum | solution.py:279
  287.5 1.9 add_bitcast_fusion
  289.4 8.3 %all-gather.3.cloned.1.call-done = bf16[6144,192]{0,1:T(8,128)(2,1)} async-done(((bf16[768,192]{0,1:T(8,128)(2,1)}), bf16[6144,192]{0,1:T(8,128)(2,1)}) %all-gather.3.cloned.1.call-update) | async-done | bytes 2359312 | tf_op jit(solution)/shard_map/all_gather | solution.py:14
  297.8 2.3 copy.75
  300.1 1.7 bitcast_reduce_fusion
  302.6 182.3 %all-reduce.7.cloned.1.call-done = (bf16[1,768,3072]{2,1,0:T(8,128)(2,1)}, bf16[1,3072,768]{2,1,0:T(8,128)(2,1)}) async-done(((bf16[1,768,3072]{2,1,0:T(8,128)(2,1)}, bf16[1,3072,768]{2,1,0:T(8,128)(2,1)}), (bf16[1,768,3072]{2,1,0:T(8,128)(2,1)}, bf16[1,3072,768]{2,1,0:T(8,128)(2,1)})) %all-reduce.7.cloned.1.call-update) | async-done | bytes 9437200 | tf_op jit(solution)/shard_map/psum | solution.py:198
  485.0 7.5 %broadcast_in_dim.113 = f32[1,768,3072]{2,1,0:T(8,128)} convert(bf16[1,768,3072]{2,1,0:T(8,128)(2,1)} %get-tuple-element.86) | non-fusion elementwise | flops 2359296 | bytes 14155776 | tf_op jit(solution)/shard_map/broadcast_in_dim | solution.py:294
  492.5 4.5 broadcast_in_dim.115
  (165 shorter events, 27.6 us)
Async XLA Ops:
  7.2 22.2 %copy-start = (bf16[192,768]{1,0:T(8,128)(2,1)S(1)}, bf16[192,768]{1,0:T(8,128)(2,1)}, u32[]{:S(2)}) copy-start(bf16[192,768]{1,0:T(8,128)(2,1)} %param.28) | copy-start | bytes 884740
  7.2 17.2 %copy-start.27 = (bf16[768,192]{0,1:T(8,128)(2,1)S(1)}, bf16[768,192]{0,1:T(8,128)(2,1)}, u32[]{:S(2)}) copy-start(bf16[768,192]{0,1:T(8,128)(2,1)} %param.27) | copy-start | bytes 884740
  7.2 52.7 %reduce-scatter.3.cloned.1.call-start = ((), (), s32[]{:S(2)}) async-start(), calls=%async_computation.6 | async-start | bytes 1966080 | tf_op jit(solution)/shard_map/reduce_scatter | solution.py:136
  12.2 14.0 %copy-start.33 = (s32[1,512]{1,0:T(1,128)S(1)}, s32[1,512]{1,0:T(1,128)}, u32[]{:S(2)}) copy-start(s32[1,512]{1,0:T(1,128)} %param.19) | copy-start | bytes 6148
  22.3 4.2 copy-start.22
  26.1 1.4 copy-start.15
  26.1 1.9 copy-start.20
  28.7 2.2 copy-start.35
  28.7 6.2 %copy-start.36 = (f32[1,128,2]{1,2,0:T(2,128)S(1)}, f32[1,128,2]{1,2,0:T(2,128)}, u32[]{:S(2)}) copy-start(f32[1,128,2]{1,2,0:T(2,128)} %param.22) | copy-start | bytes 3076
  36.3 25.5 %copy-start.32 = (f32[768]{0:T(1024)S(1)}, f32[768]{0:T(1024)}, u32[]{:S(2)}) copy-start(f32[768]{0:T(1024)} %param.29) | copy-start | bytes 9220
  36.3 25.5 %copy-start.34 = (f32[768]{0:T(1024)S(1)}, f32[768]{0:T(1024)}, u32[]{:S(2)}) copy-start(f32[768]{0:T(1024)} %param.30) | copy-start | bytes 9220
  38.7 24.5 %all-to-all-start.2 = ((bf16[2,2,128,768]{3,2,1,0:T(8,128)(2,1)}), bf16[2,2,128,768]{3,2,1,0:T(8,128)(2,1)}, u32[]{:S(2)}, u32[]{:S(2)}) async-start(bf16[2,2,128,768]{3,2,1,0:T(8,128)(2,1)} %bitcast.219), calls=%async_computation.3 | async-start | bytes 1572864 | tf_op jit(solution)/shard_map/all_to_all | solution.py:45
  63.2 15.3 %all-to-all-start = ((bf16[2,2,128,768]{3,2,1,0:T(8,128)(2,1)}), bf16[2,2,128,768]{3,2,1,0:T(8,128)(2,1)}, u32[]{:S(2)}, u32[]{:S(2)}) async-start(bf16[2,2,128,768]{3,2,1,0:T(8,128)(2,1)} %bitcast.218), calls=%async_computation.1 | async-start | bytes 1572864 | tf_op jit(solution)/shard_map/all_to_all | solution.py:45
  78.6 12.4 %slice-start.4 = ((s8[4718592]{0:T(1024)(128)(4,1)}), s8[4194304]{0:T(1024)(128)(4,1)S(1)}, s32[]{:S(2)}) async-start(s8[4718592]{0:T(1024)(128)(4,1)} %bitcast.251), calls=%async_computation.15 | async-start | bytes 8388608
  78.6 14.5 %slice-start = ((s8[4718592]{0:T(1024)(128)(4,1)}), s8[4194304]{0:T(1024)(128)(4,1)S(1)}, s32[]{:S(2)}) async-start(s8[4718592]{0:T(1024)(128)(4,1)} %bitcast.247), calls=%async_computation.11 | async-start | bytes 8388608
  78.6 16.0 %slice-start.2 = ((s8[4718592]{0:T(1024)(128)(4,1)}), s8[4194304]{0:T(1024)(128)(4,1)S(1)}, s32[]{:S(2)}) async-start(s8[4718592]{0:T(1024)(128)(4,1)} %bitcast.249), calls=%async_computation.13 | async-start | bytes 8388608
  79.9 14.6 %copy-start.11 = (bf16[2,1,128,768]{3,2,1,0:T(8,128)(2,1)}, bf16[2,1,128,768]{3,2,1,0:T(8,128)(2,1)S(1)}, u32[]{:S(2)}) copy-start(bf16[2,1,128,768]{3,2,1,0:T(8,128)(2,1)S(1)} %get-tuple-element.105) | copy-start | bytes 1179652
  79.9 11.1 %copy-start.26 = (bf16[2,1,128,768]{3,2,1,0:T(8,128)(2,1)S(1)}, bf16[2,1,128,768]{3,2,1,0:T(8,128)(2,1)}, u32[]{:S(2)}) copy-start(bf16[2,1,128,768]{3,2,1,0:T(8,128)(2,1)} %get-tuple-element.102) | copy-start | bytes 1179652
  79.9 11.1 %slice-start.5 = ((s8[4718592]{0:T(1024)(128)(4,1)}), s8[524288]{0:T(1024)(128)(4,1)S(1)}, s32[]{:S(2)}) async-start(s8[4718592]{0:T(1024)(128)(4,1)} %bitcast.251), calls=%async_computation.16 | async-start | bytes 1048576
  79.9 13.1 %slice-start.1 = ((s8[4718592]{0:T(1024)(128)(4,1)}), s8[524288]{0:T(1024)(128)(4,1)S(1)}, s32[]{:S(2)}) async-start(s8[4718592]{0:T(1024)(128)(4,1)} %bitcast.247), calls=%async_computation.12 | async-start | bytes 1048576
  79.9 14.6 %slice-start.3 = ((s8[4718592]{0:T(1024)(128)(4,1)}), s8[524288]{0:T(1024)(128)(4,1)S(1)}, s32[]{:S(2)}) async-start(s8[4718592]{0:T(1024)(128)(4,1)} %bitcast.249), calls=%async_computation.14 | async-start | bytes 1048576
  93.1 10.5 %slice-start.6 = ((s8[4718592]{0:T(1024)(128)(4,1)}), s8[4194304]{0:T(1024)(128)(4,1)S(1)}, s32[]{:S(2)}) async-start(s8[4718592]{0:T(1024)(128)(4,1)} %bitcast.253), calls=%async_computation.17 | async-start | bytes 8388608
  94.5 9.0 %copy-start.17 = (bf16[2,1,128,768]{3,2,1,0:T(8,128)(2,1)S(1)}, bf16[2,1,128,768]{3,2,1,0:T(8,128)(2,1)}, u32[]{:S(2)}) copy-start(bf16[2,1,128,768]{3,2,1,0:T(8,128)(2,1)} %get-tuple-element.103) | copy-start | bytes 1179652
  94.6 9.0 %slice-start.7 = ((s8[4718592]{0:T(1024)(128)(4,1)}), s8[524288]{0:T(1024)(128)(4,1)S(1)}, s32[]{:S(2)}) async-start(s8[4718592]{0:T(1024)(128)(4,1)} %bitcast.253), calls=%async_computation.18 | async-start | bytes 1048576
  105.6 1.5 copy-start.19
  108.1 14.4 %all-to-all-start.3 = ((bf16[2,2,128,768]{3,2,1,0:T(8,128)(2,1)}), bf16[2,2,128,768]{3,2,1,0:T(8,128)(2,1)}, u32[]{:S(2)}, u32[]{:S(2)}) async-start(bf16[2,2,128,768]{3,2,1,0:T(8,128)(2,1)} %copy.66), calls=%async_computation.4 | async-start | bytes 1572864 | tf_op jit(solution)/shard_map/all_to_all | solution.py:49
  112.4 105.6 %all-reduce.9.cloned.1.call-start = ((), (), s32[]{:S(2)}) async-start(), calls=%async_computation.10 | async-start | bytes 1769472 | tf_op jit(solution)/shard_map/psum | solution.py:271
  122.6 3.2 copy-start.2
  122.6 4.2 copy-start.9
  122.6 12.1 %copy-start.25 = (bf16[3,512,64]{1,2,0:T(8,128)(2,1)S(1)}, bf16[3,512,64]{1,2,0:T(8,128)(2,1)}, u32[]{:S(2)}) copy-start(bf16[3,512,64]{1,2,0:T(8,128)(2,1)} %copy-done.24) | copy-start | bytes 589828
  134.7 2.1 copy-start.21
  136.8 2.7 copy-start.28
  137.5 1.5 copy-start.14
  139.4 1.8 copy-start.30
  141.1 3.7 copy-start.12
  141.2 101.5 %reduce-scatter.5.cloned.1.call-start = ((), (), s32[]{:S(2)}) async-start(), calls=%async_computation.7 | async-start | bytes 983040 | tf_op jit(solution)/shard_map/reduce_scatter | solution.py:259
  143.9 153.9 %all-gather.3.cloned.1.call-start = ((), (), s32[]{:S(2)}) async-start(), calls=%async_computation.8 | async-start | bytes 2654208 | tf_op jit(solution)/shard_map/all_gather | solution.py:14
  144.5 5.5 %copy-start.6 = (bf16[256,3072]{1,0:T(8,128)(2,1)S(1)}, bf16[256,3072]{1,0:T(8,128)(2,1)}, u32[]{:S(2)}) copy-start(bf16[256,3072]{1,0:T(8,128)(2,1)} %get-tuple-element.95) | copy-start | bytes 4718596
  144.5 5.5 %copy-start.18 = (bf16[2,1,128,768]{3,2,1,0:T(8,128)(2,1)S(1)}, bf16[2,1,128,768]{3,2,1,0:T(8,128)(2,1)}, u32[]{:S(2)}) copy-start(bf16[2,1,128,768]{3,2,1,0:T(8,128)(2,1)} %get-tuple-element.103) | copy-start | bytes 1179652
  144.5 340.4 %all-reduce.7.cloned.1.call-start = ((), (), s32[]{:S(2)}) async-start(), calls=%async_computation.9 | async-start | bytes 18874368 | tf_op jit(solution)/shard_map/psum | solution.py:198
  153.7 1.4 copy-start.37
  162.6 16.5 %copy-start.3 = (f32[128,768]{1,0:T(8,128)S(1)}, f32[128,768]{1,0:T(8,128)}, u32[]{:S(2)}) copy-start(f32[128,768]{1,0:T(8,128)} %copy-done.1) | copy-start | bytes 1179652
  163.6 15.1 %all-to-all-start.1 = ((bf16[2,2,128,768]{3,2,1,0:T(8,128)(2,1)}), bf16[2,2,128,768]{3,2,1,0:T(8,128)(2,1)S(1)}, u32[]{:S(2)}, u32[]{:S(2)}) async-start(bf16[2,2,128,768]{3,2,1,0:T(8,128)(2,1)} %copy.65), calls=%async_computation.2 | async-start | bytes 1572864 | tf_op jit(solution)/shard_map/all_to_all | solution.py:49
  167.2 75.5 %copy-start.4 = (bf16[1,128,768]{2,1,0:T(8,128)(2,1)S(1)}, bf16[1,128,768]{2,1,0:T(8,128)(2,1)}, u32[]{:S(2)}) copy-start(bf16[1,128,768]{2,1,0:T(8,128)(2,1)} %param.18) | copy-start | bytes 589828
  167.2 75.5 %copy-start.31 = (f32[768]{0:T(1024)S(1)}, f32[768]{0:T(1024)}, u32[]{:S(2)}) copy-start(f32[768]{0:T(1024)} %param.23) | copy-start | bytes 9220
  178.7 108.8 %copy-start.8 = (f32[128,768]{1,0:T(8,128)S(1)}, f32[128,768]{1,0:T(8,128)}, u32[]{:S(2)}) copy-start(f32[128,768]{1,0:T(8,128)} %copy-done.7) | copy-start | bytes 1179652
  178.7 108.8 %copy-start.10 = (bf16[1,128,768]{2,1,0:T(8,128)(2,1)S(1)}, bf16[1,128,768]{2,1,0:T(8,128)(2,1)}, u32[]{:S(2)}) copy-start(bf16[1,128,768]{2,1,0:T(8,128)(2,1)} %param.35) | copy-start | bytes 589828
  485.0 7.5 %copy-start.5 = (bf16[1,3072,768]{2,1,0:T(8,128)(2,1)S(1)}, bf16[1,3072,768]{2,1,0:T(8,128)(2,1)}, u32[]{:S(2)}) copy-start(bf16[1,3072,768]{2,1,0:T(8,128)(2,1)} %get-tuple-element.87) | copy-start | bytes 14155780
  (7 other events, 5.8 us)
Sparse Core Ops, SparseCore 0:
  31.1 28.8 reduce-scatter.2
  141.3 76.6 all-reduce.8
  220.5 22.0 reduce-scatter.4
  244.8 52.9 all-gather.2
  301.9 183.0 all-reduce.6
